TPU v7x, 32 devices: a whole 2x2x4 slice. The times are simulated.
32 devices in a mesh: lat: 4 (over x, core), lon: 8 (over z, y).
Axes of the slice: x: 2, y: 2, z: 4, core: 2. Of those that a mesh axis runs over, the one named last changes fastest.
Arguments:
- start_state: float32 [256, 64, 1024], P('lat', None, 'lon'), may hold values from -6 to 6
- coefficients: float32 [5, 64], replicated, may hold values from 0.05 to 0.35
- w_in: bfloat16 [64, 512], replicated, may hold values from -0.75 to 0.75
- w_out: bfloat16 [512, 64], replicated, may hold values from -0.25 to 0.25
- jacobian: float32 [128, 64], replicated, may hold values from -0.75 to 0.75
- sigma: float32 [128], replicated, may hold values from 0.5 to 2
- obs_values: float32 [8192, 128], P(('lat', 'lon')), may hold values from -6 to 6
- owner: int32 [8192, 1], P(('lat', 'lon')), may hold values from 0 to 31; in each aligned block of 256 rows (0 to 255, 256 to 511, ...) at most 16 rows name the same one
- stencil: int32 [8192, 4], P(('lat', 'lon')), may hold values from 0 to 8191
- counts: int32 [8192], P(('lat', 'lon')), may hold values from 1 to 128
Outputs:
- grad_state: float32 [256, 64, 1024], P('lat', None, 'lon')
- departures: float32 [8192, 128], P(('lat', 'lon'))
- grad_w_in: float32 [64, 512], replicated
- grad_w_out: float32 [512, 64], replicated
Inputs may be any that keep to these rules, and one draw needn't show every extreme that they name: owner is the tile's index lat * 8 + lon. Among the rows of one device no tile is named by more than 16 rows, a bound that some block reaches. `stencil`: A cell index inside the owning tile is its row times 128 plus its column.
All inputs are finite; a program needn't handle non-finite values.
Results may differ from a plain program's by a relative error of at most 0.0018.
The roundings to bfloat16 on the way count: a program that leaves them out, or rounds other values in their place, can miss the bound.
Values sent between devices are 32-bit elements; how exact they have to be, the bound alone decides.
A program may use at most 128 MiB of HBM per device.

v0:
```python
import math
import jax
import jax.numpy as jnp
from jax import lax
from jax.sharding import PartitionSpec as P

CAP = 16
interp_weights = (0.4, 0.3, 0.2, 0.1)


def padded(shard, sides, width, wrap):
    for axis, dim in sides:
        peers, length = (lax.axis_size(axis), shard.shape[dim])
        up = [(i, (i + 1) % peers) for i in range(peers if wrap else peers - 1)]
        down = [(j, i) for i, j in up]
        last = lax.slice_in_dim(shard, length - width, length, axis=dim)
        initial = lax.slice_in_dim(shard, 0, width, axis=dim)
        before = lax.ppermute(last, axis, up)
        after = lax.ppermute(initial, axis, down)
        shard = jnp.concatenate([before, shard, after], axis=dim)
    return shard


def group_size(nrows, width, target):
    group = max(1, min(nrows, target // width))
    while nrows % group:
        group -= 1
    return group


def stencil_apply(extended, coefficients):
    scaled = coefficients[:, None, :, None]
    centre = extended[1:-1, :, 1:-1]
    return (
        scaled[0] * centre
        + scaled[1] * extended[:-2, :, 1:-1]
        + scaled[2] * extended[2:, :, 1:-1]
        + scaled[3] * extended[1:-1, :, :-2]
        + scaled[4] * extended[1:-1, :, 2:]
    )


def stencil_adjoint(extended, coefficients):
    scaled = coefficients[:, None, :, None]
    centre = extended[1:-1, :, 1:-1]
    return (
        scaled[0] * centre
        + scaled[1] * extended[2:, :, 1:-1]
        + scaled[2] * extended[:-2, :, 1:-1]
        + scaled[3] * extended[1:-1, :, 2:]
        + scaled[4] * extended[1:-1, :, :-2]
    )


def closure_block(block, w_in, w_out):
    inputs = block.astype(jnp.bfloat16)
    pre = jnp.einsum("fh,gfw->ghw", w_in, inputs, preferred_element_type=jnp.float32)
    hidden = jnp.tanh(pre).astype(jnp.bfloat16)
    return jnp.einsum("hf,ghw->gfw", w_out, hidden, preferred_element_type=jnp.float32)


def closure_forward(state, w_in, w_out):
    nrows, feat, width = state.shape
    group = group_size(nrows, width, 2048)
    blocks = state.reshape(nrows // group, group, feat, width)
    result = lax.map(lambda block: closure_block(block, w_in, w_out), blocks)
    return result.reshape(nrows, feat, width)


def closure_backward(state, cotangent, w_in, w_out):
    nrows, feat, width = state.shape
    group = group_size(nrows, width, 2048)
    blocks = state.reshape(nrows // group, group, feat, width)
    cot_blocks = cotangent.reshape(nrows // group, group, feat, width)

    def one_block(carry, pieces):
        block, cot_block = pieces
        inputs = block.astype(jnp.bfloat16)
        pre = jnp.einsum("fh,gfw->ghw", w_in, inputs, preferred_element_type=jnp.float32)
        tanh_pre = jnp.tanh(pre)
        hidden = tanh_pre.astype(jnp.bfloat16)
        cot_low = cot_block.astype(jnp.bfloat16)
        grad_out = jnp.einsum("ghw,gfw->hf", hidden, cot_low, preferred_element_type=jnp.float32)
        back_hidden = jnp.einsum("hf,gfw->ghw", w_out, cot_low, preferred_element_type=jnp.float32)
        back_pre = (back_hidden * (1.0 - tanh_pre * tanh_pre)).astype(jnp.bfloat16)
        grad_in = jnp.einsum("gfw,ghw->fh", inputs, back_pre, preferred_element_type=jnp.float32)
        back_state = jnp.einsum("fh,ghw->gfw", w_in, back_pre, preferred_element_type=jnp.float32)
        return ((carry[0] + grad_in, carry[1] + grad_out), back_state)

    init = (
        jnp.zeros((feat, w_in.shape[1]), jnp.float32),
        jnp.zeros((w_in.shape[1], feat), jnp.float32),
    )
    totals, back = lax.scan(one_block, init, (blocks, cot_blocks))
    return (back.reshape(nrows, feat, width), totals[0], totals[1])


def extend_forward(state):
    wider = padded(state, (("lon", 2),), 1, True)
    return padded(wider, (("lat", 0),), 1, False)


def extend_adjoint(field):
    wider = padded(field, (("lon", 2),), 1, True)
    return padded(wider, (("lat", 0),), 1, False)


def interpolate(state_two, cell_rows, cell_cols):
    interp = interp_weights[0] * state_two[cell_rows[:, 0], :, cell_cols[:, 0]]
    for corner in range(1, 4):
        interp = (
            interp
            + interp_weights[corner] * state_two[cell_rows[:, corner], :, cell_cols[:, corner]]
        )
    return interp


def spread_back(like, cell_rows, cell_cols, pulled):
    adjoint_two = jnp.zeros_like(like)
    for corner in range(4):
        adjoint_two = adjoint_two.at[cell_rows[:, corner], :, cell_cols[:, corner]].add(
            interp_weights[corner] * pulled
        )
    return adjoint_two


def on_device(
    start_state, coefficients, w_in, w_out, jacobian, sigma, obs_values, owner, stencil, counts
):
    tlat, feat, tlon = start_state.shape
    lat_count = lax.axis_size("lat")
    lon_count = lax.axis_size("lon")
    devices = lat_count * lon_count
    channels = obs_values.shape[1]
    tile_owner = owner[:, 0]
    onehot = (tile_owner[:, None] == jnp.arange(devices, dtype=jnp.int32)[None, :]).astype(
        jnp.int32
    )
    running = jnp.cumsum(onehot, axis=0)
    rank = jnp.sum(running * onehot, axis=1) - 1
    slot = tile_owner * CAP + rank
    slots = devices * CAP
    send_stencil = jnp.zeros((slots, 4), jnp.int32).at[slot].set(stencil)
    channel_ids = jnp.arange(channels, dtype=jnp.int32)
    cell_recv = lax.all_to_all(
        send_stencil, ("lat", "lon"), split_axis=0, concat_axis=0, tiled=True
    )
    state_one = stencil_apply(extend_forward(start_state), coefficients) + closure_forward(
        start_state, w_in, w_out
    )
    state_two = stencil_apply(extend_forward(state_one), coefficients) + closure_forward(
        state_one, w_in, w_out
    )
    cell_rows = cell_recv // tlon
    cell_cols = cell_recv % tlon
    slot_interp = interpolate(state_two, cell_rows, cell_cols)
    returned_interp = lax.all_to_all(
        slot_interp, ("lat", "lon"), split_axis=0, concat_axis=0, tiled=True
    )
    row_interp = returned_interp[slot]
    evolved = jnp.dot(
        row_interp, jacobian.T, precision=lax.Precision.HIGHEST, preferred_element_type=jnp.float32
    )
    used = channel_ids[None, :] < counts[:, None]
    departures = jnp.where(used, (obs_values - evolved) / sigma[None, :], 0.0)
    row_pulled = jnp.dot(
        -departures / sigma[None, :],
        jacobian,
        precision=lax.Precision.HIGHEST,
        preferred_element_type=jnp.float32,
    )
    send_pulled = jnp.zeros((slots, feat), jnp.float32).at[slot].set(row_pulled)
    recv_pulled = lax.all_to_all(
        send_pulled, ("lat", "lon"), split_axis=0, concat_axis=0, tiled=True
    )
    adjoint_two = spread_back(state_two, cell_rows, cell_cols, recv_pulled)
    back_one, gin_one, gout_one = closure_backward(state_one, adjoint_two, w_in, w_out)
    adjoint_one = stencil_adjoint(extend_adjoint(adjoint_two), coefficients) + back_one
    back_zero, gin_zero, gout_zero = closure_backward(start_state, adjoint_one, w_in, w_out)
    grad_state = stencil_adjoint(extend_adjoint(adjoint_one), coefficients) + back_zero
    grad_in, grad_out = lax.psum((gin_one + gin_zero, gout_one + gout_zero), ("lat", "lon"))
    scale = 1.0 / math.sqrt(tlat * lat_count * tlon * lon_count)
    return (grad_state, departures, grad_in * scale, grad_out * scale)


def solution(mesh):
    return jax.shard_map(
        on_device,
        mesh=mesh,
        in_specs=(
            P("lat", None, "lon"),
            P(),
            P(),
            P(),
            P(),
            P(),
            P(("lat", "lon"), None),
            P(("lat", "lon"), None),
            P(("lat", "lon"), None),
            P(("lat", "lon")),
        ),
        out_specs=(P("lat", None, "lon"), P(("lat", "lon"), None), P(), P()),
        check_vma=False,
    )
```

profile of v0, /device:TPU:0, one launch (start us, length us, event | category | flops | bytes accessed | tf_op | source)
XLA Modules:
  0.0 732.3 jit_solution(17670146646272283155)
XLA Ops:
  7.2 3.9 copy.71
  25.4 5.4 while.50
  41.5 6.1 fusion.139
  59.1 4.3 collective-permute-start.6
  66.5 8.5 %while.51 = (s32[]{:T(128)}, f32[4,16,64,128]{3,2,1,0:T(8,128)}, bf16[4,16,64,128]{3,2,1,0:T(8,128)(2,1)S(1)}, bf16[64,512]{1,0:T(8,128)(2,1)S(1)}, bf16[512,64]{0,1:T(8,128)(2,1)S(1)}, /*index=5*/s32[]{:T(128)}) while((s32[]{:T(128)}, f32[4,16,64,128]{3,2,1,0:T(8,128)}, bf16[4,16,64,128]{3,2,1,0:T(8,128)(2,1)S(1)}, ...), condition=%wide.region_7.8_spmd, body=%wide.region_6.7_spmd.sunk | while | flops 269484032 | bytes 918597 | solution.py:66
  75.0 3.8 copy.79
  78.8 14.8 %fusion.130 = f32[64,64,128]{1,2,0:T(8,128)} fusion(f32[64,64,1]{1,2,0:T(1,128)S(1)} %collective-permute-done.5, f32[64,64,128]{1,2,0:T(8,128)} %copy-done.5, f32[64,64,1]{1,2,0:T(1,128)S(1)} %collective-permute-done.4, f32[1,64,130]{1,2,0:T(8,128)S(1)} %collective-permute-done.7, f32[1,64,130]{1,2,0:T(8,128)S(1)} %collective-permute-done.6, ...), kind=kLoop, calls=%fused_computation.120 | loop fusion | flops 9437184 | bytes 6392064 | tf_op jit(solution)/shard_map/add | solution.py:151
  93.6 6.0 gather_fusion
  99.5 6.0 gather_fusion.1
  105.5 6.0 gather_fusion.2
  111.5 8.4 %gather_fusion.3 = f32[512,64]{1,0:T(8,128)} fusion(f32[64,64,128]{1,2,0:T(8,128)} %fusion.130, s32[512]{0:T(512)S(1)} %get-tuple-element.284), kind=kCustom, calls=%fused_computation.3 | custom fusion | bytes 266240 | tf_op jit(solution)/shard_map/gather | solution.py:113
  123.4 47.9 %all-to-all-start.1 = ((f32[32,1,1024]{2,1,0:T(1,128)}), f32[32,1,1024]{2,1,0:T(1,128)S(1)}, u32[]{:S(2)}, u32[]{:S(2)}) async-start(f32[32,1,1024]{2,1,0:T(1,128)} %reshape.217), calls=%async_computation.1 | async-start | bytes 262144 | tf_op jit(solution)/shard_map/all_to_all | solution.py:157
  171.4 7.7 %all-to-all-done.1 = f32[32,1,1024]{2,1,0:T(1,128)S(1)} async-done(((f32[32,1,1024]{2,1,0:T(1,128)}), f32[32,1,1024]{2,1,0:T(1,128)S(1)}, u32[]{:S(2)}, u32[]{:S(2)}) %all-to-all-start.1) | async-done | bytes 131104 | tf_op jit(solution)/shard_map/all_to_all | solution.py:157
  184.0 10.0 %all_to_all.30 = f32[32,1,1024]{2,1,0:T(1,128)S(1)} all-to-all(f32[32,1,1024]{2,1,0:T(1,128)S(1)} %reshape.219), channel_id=1, replica_groups=mesh['lat'=4,'lon'=8] {'lat','lon'}, dimensions={0} | all-to-all | bytes 262144 | tf_op jit(solution)/shard_map/all_to_all | solution.py:173
  200.0 52.6 %scatter_fusion = f32[64,64,128]{1,2,0:T(8,128)} fusion(f32[64,64,128]{1,2,0:T(8,128)} %broadcast_in_dim.20, s32[512]{0:T(512)S(1)} %get-tuple-element.290, f32[512,64]{1,0:T(8,128)} %bitcast.306), kind=kCustom, calls=%fused_computation.7 | custom fusion | flops 32768 | bytes 397312 | tf_op jit(solution)/shard_map/scatter-add | solution.py:121
  252.6 52.2 %scatter_fusion.1 = f32[64,64,128]{1,2,0:T(8,128)} fusion(f32[64,64,128]{1,2,0:T(8,128)} %scatter_fusion, s32[512]{0:T(512)S(1)} %get-tuple-element.289, f32[512,64]{1,0:T(8,128)S(1)} %bitcast.305), kind=kCustom, calls=%fused_computation.8 | custom fusion | flops 32768 | bytes 397312 | tf_op jit(solution)/shard_map/scatter-add | solution.py:121
  304.8 52.3 %scatter_fusion.2 = f32[64,64,128]{1,2,0:T(8,128)} fusion(f32[64,64,128]{1,2,0:T(8,128)} %scatter_fusion.1, s32[512]{0:T(512)S(1)} %get-tuple-element.288, f32[512,64]{1,0:T(8,128)S(1)} %bitcast.304), kind=kCustom, calls=%fused_computation.9 | custom fusion | flops 32768 | bytes 397312 | tf_op jit(solution)/shard_map/scatter-add | solution.py:121
  357.1 52.2 %scatter_fusion.3 = f32[64,64,128]{1,2,0:T(8,128)} fusion(f32[64,64,128]{1,2,0:T(8,128)} %scatter_fusion.2, s32[512]{0:T(512)S(1)} %get-tuple-element.283, f32[512,64]{1,0:T(8,128)S(1)} %bitcast.303), kind=kCustom, calls=%fused_computation.10 | custom fusion | flops 32768 | bytes 397312 | tf_op jit(solution)/shard_map/scatter-add | solution.py:121
  410.3 46.2 %collective-permute-start.8 = (f32[64,64,1]{1,2,0:T(1,128)S(1)}, f32[64,64,1]{1,2,0:T(1,128)S(1)}, u32[]{:S(2)}, u32[]{:S(2)}) collective-permute-start(f32[64,64,1]{1,2,0:T(1,128)S(1)} %get-tuple-element.356), channel_id=1, source_target_pairs={{0,1},{1,2},{2,3},{3,4},{4,5},{5,6},{6,7},{7,0},{8,9},{9,10},{10,1... | collective-permute-start | bytes 49160 | tf_op jit(solution)/shard_map/ppermute | solution.py:18
  468.4 45.2 %while.52 = (s32[]{:T(128)}, f32[64,512]{1,0:T(8,128)S(1)}, f32[512,64]{0,1:T(8,128)}, f32[4,16,64,128]{3,2,1,0:T(8,128)}, bf16[4,16,64,128]{3,2,1,0:T(8,128)(2,...) while((s32[]{:T(128)}, f32[64,512]{1,0:T(8,128)S(1)}, ...), condition=%wide.region_14.15_spmd.clone, body=%wide.region_13.14_spmd.clone.sunk | while | flops 676462592 | bytes 46336196 | solution.py:94
  475.9 3.8 fusion.242
  487.2 3.8 fusion.242
  498.5 3.8 fusion.242
  509.8 3.8 fusion.242
  513.6 3.8 copy.83
  517.5 13.3 %fusion.121 = f32[64,64,128]{1,2,0:T(8,128)S(1)} fusion(f32[64,64,128]{1,2,0:T(8,128)} %scatter_fusion.3, f32[64,64,1]{1,2,0:T(1,128)S(1)} %collective-permute-done.8, f32[64,64,1]{1,2,0:T(1,128)S(1)} %collective-permute-done.9, f32[1,64,130]{1,2,0:T(8,128)} %collective-permute-done.11, f32[1,64,130]{1,2,0:T(8,128)} %collective-permute-done.10, ...), kind=kLoop, calls=%fused_computation.103 | loop fusion | flops 9437184 | bytes 6392064 | tf_op jit(solution)/shard_map/add | solution.py:178
  549.1 41.2 %while.53 = (s32[]{:T(128)}, f32[64,512]{1,0:T(8,128)S(1)}, f32[512,64]{0,1:T(8,128)}, f32[4,16,64,128]{3,2,1,0:T(8,128)}, bf16[4,16,64,128]{3,2,1,0:T(8,128)(2,...) while((s32[]{:T(128)}, f32[64,512]{1,0:T(8,128)S(1)}, ...), condition=%wide.region_16.17_spmd.clone, body=%wide.region_15.16_spmd.clone.sunk | while | flops 676462592 | bytes 37947028 | solution.py:94
  555.7 3.7 fusion.256
  590.3 3.9 copy.85
  595.6 14.6 %fusion.112 = f32[64,64,128]{1,2,0:T(8,128)} fusion(f32[64,64,128]{1,2,0:T(8,128)} %copy-done.4, f32[64,64,1]{1,2,0:T(1,128)S(1)} %collective-permute-done.12, f32[64,64,1]{1,2,0:T(1,128)S(1)} %collective-permute-done.13, f32[1,64,130]{1,2,0:T(8,128)} %collective-permute-done.15, f32[1,64,130]{1,2,0:T(8,128)} %collective-permute-done.14, ...), kind=kLoop, calls=%fused_computation.86 | loop fusion | flops 9437184 | bytes 6392064 | tf_op jit(solution)/shard_map/add | solution.py:180
  610.2 3.8 copy.86
  614.0 108.3 %all-reduce.3.cloned.1.call-done = (f32[64,512]{1,0:T(8,128)}, f32[512,64]{0,1:T(8,128)}) async-done(((f32[64,512]{1,0:T(8,128)}, f32[512,64]{0,1:T(8,128)}), (f32[64,512]{1,0:T(8,128)}, f32[512,64]{0,1:T(8,128)})) %all-reduce.3.cloned.1.call-update) | async-done | bytes 262160 | tf_op jit(solution)/shard_map/psum | solution.py:181
  (214 shorter events, 170.5 us)
Async XLA Ops:
  7.2 174.3 %copy-start = (f32[128,64]{0,1:T(8,128)S(1)}, f32[128,64]{0,1:T(8,128)}, u32[]{:S(2)}) copy-start(f32[128,64]{0,1:T(8,128)} %param.22) | copy-start | bytes 98308
  7.2 17.7 %copy-start.10 = (f32[64,64,128]{2,1,0:T(8,128)S(1)}, f32[64,64,128]{2,1,0:T(8,128)}, u32[]{:S(2)}) copy-start(f32[64,64,128]{2,1,0:T(8,128)} %param.18) | copy-start | bytes 6291460
  7.2 11.2 %copy-start.22 = (s32[256,1]{0,1:T(1,128)S(1)}, s32[256,1]{0,1:T(1,128)}, u32[]{:S(2)}) copy-start(s32[256,1]{0,1:T(1,128)} %param.25) | copy-start | bytes 3076
  7.2 12.2 %copy-start.23 = (s32[256,4]{0,1:T(4,128)S(1)}, s32[256,4]{0,1:T(4,128)}, u32[]{:S(2)}) copy-start(s32[256,4]{0,1:T(4,128)} %param.26) | copy-start | bytes 12292
  11.1 14.2 %copy-start.7 = (bf16[64,512]{1,0:T(8,128)(2,1)S(1)}, bf16[64,512]{1,0:T(8,128)(2,1)}, u32[]{:S(2)}) copy-start(bf16[64,512]{1,0:T(8,128)(2,1)} %param.20) | copy-start | bytes 196612
  11.1 14.2 %copy-start.11 = (bf16[512,64]{0,1:T(8,128)(2,1)S(1)}, bf16[512,64]{0,1:T(8,128)(2,1)}, u32[]{:S(2)}) copy-start(bf16[512,64]{0,1:T(8,128)(2,1)} %param.21) | copy-start | bytes 196612
  12.3 21.6 %collective-permute-start = (f32[64,64,1]{1,2,0:T(1,128)S(1)}, f32[64,64,1]{1,2,0:T(1,128)S(1)}, u32[]{:S(2)}, u32[]{:S(2)}) collective-permute-start(f32[64,64,1]{1,2,0:T(1,128)S(1)} %get-tuple-element.359), channel_id=1, source_target_pairs={{0,1},{1,2},{2,3},{3,4},{4,5},{5,6},{6,7},{7,0},{8,9},{9,10},{10,1... | collective-permute-start | bytes 49160 | tf_op jit(solution)/shard_map/ppermute | solution.py:18
  15.3 18.5 %collective-permute-start.1 = (f32[64,64,1]{1,2,0:T(1,128)S(1)}, f32[64,64,1]{1,2,0:T(1,128)S(1)}, u32[]{:S(2)}, u32[]{:S(2)}) collective-permute-start(f32[64,64,1]{1,2,0:T(1,128)S(1)} %get-tuple-element.360), channel_id=1, source_target_pairs={{1,0},{2,1},{3,2},{4,3},{5,4},{6,5},{7,6},{0,7},{9,8},{10,9},{11,1... | collective-permute-start | bytes 49160 | tf_op jit(solution)/shard_map/ppermute | solution.py:19
  21.6 11.9 %all-to-all-start = ((s32[32,16,4]{1,2,0:T(4,128)}), s32[32,16,4]{1,2,0:T(4,128)S(1)}, u32[]{:S(2)}, u32[]{:S(2)}) async-start(s32[32,16,4]{1,2,0:T(4,128)} %copy.69), calls=%async_computation | async-start | bytes 131072 | tf_op jit(solution)/shard_map/all_to_all | solution.py:145
  30.8 48.0 %copy-start.16 = (f32[64]{0:T(128)}, f32[64]{0:T(128)S(1)}, u32[]{:S(2)}) copy-start(f32[64]{0:T(128)S(1)} %get-tuple-element.372) | copy-start | bytes 772
  30.8 48.0 %copy-start.19 = (f32[64]{0:T(128)}, f32[64]{0:T(128)S(1)}, u32[]{:S(2)}) copy-start(f32[64]{0:T(128)S(1)} %get-tuple-element.373) | copy-start | bytes 772
  34.9 3.8 collective-permute-start.2
  37.2 4.3 collective-permute-start.3
  49.6 8.6 %collective-permute-start.4 = (f32[64,64,1]{1,2,0:T(1,128)S(1)}, f32[64,64,1]{1,2,0:T(1,128)S(1)}, u32[]{:S(2)}, u32[]{:S(2)}) collective-permute-start(f32[64,64,1]{1,2,0:T(1,128)S(1)} %get-tuple-element.357), channel_id=1, source_target_pairs={{0,1},{1,2},{2,3},{3,4},{4,5},{5,6},{6,7},{7,0},{8,9},{9,10},{10,1... | collective-permute-start | bytes 49160 | tf_op jit(solution)/shard_map/ppermute | solution.py:18
  51.1 7.1 collective-permute-start.5
  59.1 19.7 %collective-permute-start.6 = (f32[1,64,130]{1,2,0:T(8,128)S(1)}, f32[1,64,130]{1,2,0:T(8,128)S(1)}, u32[]{:S(2)}, u32[]{:S(2)}) collective-permute-start(f32[1,64,130]{1,2,0:T(8,128)S(1)} %get-tuple-element.349), channel_id=1, source_target_pairs={{0,8},{8,16},{16,24},{1,9},{9,17},{17,25},{2,10},{10,18},{18,26},{... | collective-permute-start | bytes 99848 | tf_op jit(solution)/shard_map/ppermute | solution.py:18
  63.4 15.3 %collective-permute-start.7 = (f32[1,64,130]{1,2,0:T(8,128)S(1)}, f32[1,64,130]{1,2,0:T(8,128)S(1)}, u32[]{:S(2)}, u32[]{:S(2)}) collective-permute-start(f32[1,64,130]{1,2,0:T(8,128)S(1)} %get-tuple-element.350), channel_id=1, source_target_pairs={{8,0},{16,8},{24,16},{9,1},{17,9},{25,17},{10,2},{18,10},{26,18},{... | collective-permute-start | bytes 99848 | tf_op jit(solution)/shard_map/ppermute | solution.py:19
  105.5 75.9 %copy-start.25 = (f32[256,128]{1,0:T(8,128)S(1)}, f32[256,128]{1,0:T(8,128)}, u32[]{:S(2)}) copy-start(f32[256,128]{1,0:T(8,128)} %param.24) | copy-start | bytes 393220
  105.5 75.9 %copy-start.26 = (s32[256]{0:T(256)S(1)}, s32[256]{0:T(256)}, u32[]{:S(2)}) copy-start(s32[256]{0:T(256)} %param.27) | copy-start | bytes 3076
  105.5 75.9 %copy-start.27 = (f32[128]{0:T(128)S(1)}, f32[128]{0:T(128)}, u32[]{:S(2)}) copy-start(f32[128]{0:T(128)} %param.23) | copy-start | bytes 1540
  123.4 55.7 %all-to-all-start.1 = ((f32[32,1,1024]{2,1,0:T(1,128)}), f32[32,1,1024]{2,1,0:T(1,128)S(1)}, u32[]{:S(2)}, u32[]{:S(2)}) async-start(f32[32,1,1024]{2,1,0:T(1,128)} %reshape.217), calls=%async_computation.1 | async-start | bytes 262144 | tf_op jit(solution)/shard_map/all_to_all | solution.py:157
  171.3 551.0 %all-reduce.3.cloned.1.call-start = ((), (), s32[]{:S(2)}) async-start(), calls=%async_computation.3 | async-start | bytes 524288 | tf_op jit(solution)/shard_map/psum | solution.py:181
  410.3 49.6 %collective-permute-start.8 = (f32[64,64,1]{1,2,0:T(1,128)S(1)}, f32[64,64,1]{1,2,0:T(1,128)S(1)}, u32[]{:S(2)}, u32[]{:S(2)}) collective-permute-start(f32[64,64,1]{1,2,0:T(1,128)S(1)} %get-tuple-element.356), channel_id=1, source_target_pairs={{0,1},{1,2},{2,3},{3,4},{4,5},{5,6},{6,7},{7,0},{8,9},{9,10},{10,1... | collective-permute-start | bytes 49160 | tf_op jit(solution)/shard_map/ppermute | solution.py:18
  456.5 3.9 collective-permute-start.9
  461.9 55.5 %collective-permute-start.10 = (f32[1,64,130]{1,2,0:T(8,128)}, f32[1,64,130]{1,2,0:T(8,128)}, u32[]{:S(2)}, u32[]{:S(2)}) collective-permute-start(f32[1,64,130]{1,2,0:T(8,128)} %get-tuple-element.347), channel_id=1, source_target_pairs={{8,0},{16,8},{24,16},{9,1},{17,9},{25,17},{10,2},{18,10},{26,18},{... | collective-permute-start | bytes 99848 | tf_op jit(solution)/shard_map/ppermute | solution.py:19
  463.2 54.3 %collective-permute-start.11 = (f32[1,64,130]{1,2,0:T(8,128)S(1)}, f32[1,64,130]{1,2,0:T(8,128)}, u32[]{:S(2)}, u32[]{:S(2)}) collective-permute-start(f32[1,64,130]{1,2,0:T(8,128)S(1)} %get-tuple-element.348), channel_id=1, source_target_pairs={{0,8},{8,16},{16,24},{1,9},{9,17},{17,25},{2,10},{10,18},{18,26},{... | collective-permute-start | bytes 99848 | tf_op jit(solution)/shard_map/ppermute | solution.py:18
  513.6 17.2 %copy-start.13 = (f32[64,512]{1,0:T(8,128)}, f32[64,512]{1,0:T(8,128)S(1)}, u32[]{:S(2)}) copy-start(f32[64,512]{1,0:T(8,128)S(1)} %get-tuple-element.150) | copy-start | bytes 393220
  532.9 8.2 %collective-permute-start.12 = (f32[64,64,1]{1,2,0:T(1,128)S(1)}, f32[64,64,1]{1,2,0:T(1,128)S(1)}, u32[]{:S(2)}, u32[]{:S(2)}) collective-permute-start(f32[64,64,1]{1,2,0:T(1,128)S(1)} %get-tuple-element.354), channel_id=1, source_target_pairs={{0,1},{1,2},{2,3},{3,4},{4,5},{5,6},{6,7},{7,0},{8,9},{9,10},{10,1... | collective-permute-start | bytes 49160 | tf_op jit(solution)/shard_map/ppermute | solution.py:18
  534.4 6.6 collective-permute-start.13
  542.6 53.0 %collective-permute-start.14 = (f32[1,64,130]{1,2,0:T(8,128)}, f32[1,64,130]{1,2,0:T(8,128)}, u32[]{:S(2)}, u32[]{:S(2)}) collective-permute-start(f32[1,64,130]{1,2,0:T(8,128)} %get-tuple-element.345), channel_id=1, source_target_pairs={{8,0},{16,8},{24,16},{9,1},{17,9},{25,17},{10,2},{18,10},{26,18},{... | collective-permute-start | bytes 99848 | tf_op jit(solution)/shard_map/ppermute | solution.py:19
  543.9 51.7 %collective-permute-start.15 = (f32[1,64,130]{1,2,0:T(8,128)}, f32[1,64,130]{1,2,0:T(8,128)}, u32[]{:S(2)}, u32[]{:S(2)}) collective-permute-start(f32[1,64,130]{1,2,0:T(8,128)} %get-tuple-element.346), channel_id=1, source_target_pairs={{0,8},{8,16},{16,24},{1,9},{9,17},{17,25},{2,10},{10,18},{18,26},{... | collective-permute-start | bytes 99848 | tf_op jit(solution)/shard_map/ppermute | solution.py:18
  595.6 129.9 %copy-start.1 = (f32[128,64]{0,1:T(8,128)S(1)}, f32[128,64]{0,1:T(8,128)}, u32[]{:S(2)}) copy-start(f32[128,64]{0,1:T(8,128)} %param.22) | copy-start | bytes 98308
  (28 other events, 83.0 us)
Sparse Core Ops, SparseCore 0:
  595.7 126.6 all-reduce.2
where the time goes:
time: 741 us; the launch traced here: 732 us
  other arithmetic  275 us (37%)
  starting transfers between devices  132 us (18%)
  waiting for transfers between devices  119 us (16%)
  local copies, waits for them, and re-layouts  95.7 us (13%)
  matrix products  84.7 us (11%)
  between operations  14.6 us (2%)
  blocking collectives  9.98 us (1%)
    scatter-add x4, other arithmetic, spread_back(): adjoint_two.at[cell_rows[:, corner], :, cell_cols[:, corner]]  209 us
    psum x1, waiting for transfers between devices, on_device(): lax.psum((gin_one + gin_zero, gout_one + gout_zero), ('lat', 'lon'))  108 us
    ppermute x8, starting transfers between devices, padded(): before = lax.ppermute(last, axis, up)  66.2 us
    all_to_all x1, starting transfers between devices, on_device(): lax.all_to_all(slot_interp, ('lat', 'lon'), split_axis=0, concat_axis=0,...  47.9 us
    dot_general x8, matrix products, one_block(): jnp.einsum('ghw,gfw->hf', hidden, cot_low, preferred_element_type=jnp.flo...  30 us
    unnamed x59, local copies, waits for them, and re-layouts  22.1 us
    gather x3, local copies, waits for them, and re-layouts, interpolate(): state_two[cell_rows[:, corner], :, cell_cols[:, corner]]  20.3 us
    while x32, local copies, waits for them, and re-layouts  15.7 us
  transfers between devices with their start and end apart: 19, of which 4 were waited for; matrix products, arithmetic and copies ran while one was open for 19% of the time, Pallas kernels for 0%

commit v1 on v0

--- a/solution.py
+++ b/solution.py
@@ -178,7 +178,7 @@
     adjoint_one = stencil_adjoint(extend_adjoint(adjoint_two), coefficients) + back_one
     back_zero, gin_zero, gout_zero = closure_backward(start_state, adjoint_one, w_in, w_out)
     grad_state = stencil_adjoint(extend_adjoint(adjoint_one), coefficients) + back_zero
-    grad_in, grad_out = lax.psum((gin_one + gin_zero, gout_one + gout_zero), ("lat", "lon"))
+    grad_in, grad_out = lax.psum(lax.psum((gin_one + gin_zero, gout_one + gout_zero), "lon"), "lat")
     scale = 1.0 / math.sqrt(tlat * lat_count * tlon * lon_count)
     return (grad_state, departures, grad_in * scale, grad_out * scale)
 

time: 741 us -> 705 us (0.951)
  waiting for transfers between devices: 119 us -> 81.7 us
    psum x1 -> x2, waiting for transfers between devices: 108 us -> 68.6 us  [the longest x1 53.2 us: on_device(): lax.psum((gin_one + gin_zero, gout_one + gout_zero), 'lon')]
    unnamed x59 -> x49, local copies, waits for them, and re-layouts: 22.1 us -> 20.2 us
  transfers between devices with their start and end apart: 19 -> 20, of which waited for: 4 -> 6; matrix products, arithmetic and copies ran while one was open for 19% -> 15% of each run, Pallas kernels for 0% -> 0%
where the time goes in v1:
time: 705 us; the launch traced here: 696 us
  other arithmetic  278 us (39%)
  starting transfers between devices  130 us (18%)
  local copies, waits for them, and re-layouts  94.3 us (13%)
  matrix products  87.2 us (12%)
  waiting for transfers between devices  81.7 us (12%)
  between operations  14.6 us (2%)
  blocking collectives  9.97 us (1%)
    scatter-add x4, other arithmetic, spread_back(): adjoint_two.at[cell_rows[:, corner], :, cell_cols[:, corner]]  209 us
    ppermute x8, starting transfers between devices, padded(): before = lax.ppermute(last, axis, up)  64.6 us
    psum x1, waiting for transfers between devices, on_device(): lax.psum((gin_one + gin_zero, gout_one + gout_zero), 'lon')  53.2 us
    all_to_all x1, starting transfers between devices, on_device(): lax.all_to_all(slot_interp, ('lat', 'lon'), split_axis=0, concat_axis=0,...  47.5 us
    dot_general x8, matrix products, one_block(): jnp.einsum('ghw,gfw->hf', hidden, cot_low, preferred_element_type=jnp.flo...  29.9 us
    unnamed x49, local copies, waits for them, and re-layouts  20.2 us
    gather x3, local copies, waits for them, and re-layouts, interpolate(): state_two[cell_rows[:, corner], :, cell_cols[:, corner]]  20 us
    while x32, local copies, waits for them, and re-layouts  15.6 us
  transfers between devices with their start and end apart: 20, of which 6 were waited for; matrix products, arithmetic and copies ran while one was open for 15% of the time, Pallas kernels for 0%

profile of v1, /device:TPU:0, one launch (start us, length us, event | category | flops | bytes accessed | tf_op | source)
XLA Modules:
  0.0 696.2 jit_solution(9626330514664115735)
XLA Ops:
  7.2 3.9 copy.71
  25.4 5.4 while.50
  41.5 6.1 fusion.139
  59.1 4.3 collective-permute-start.6
  66.5 8.5 %while.51 = (s32[]{:T(128)}, f32[4,16,64,128]{3,2,1,0:T(8,128)}, bf16[4,16,64,128]{3,2,1,0:T(8,128)(2,1)S(1)}, bf16[64,512]{1,0:T(8,128)(2,1)S(1)}, bf16[512,64]{0,1:T(8,128)(2,1)S(1)}, /*index=5*/s32[]{:T(128)}) while((s32[]{:T(128)}, f32[4,16,64,128]{3,2,1,0:T(8,128)}, bf16[4,16,64,128]{3,2,1,0:T(8,128)(2,1)S(1)}, ...), condition=%wide.region_7.8_spmd, body=%wide.region_6.7_spmd.sunk | while | flops 269484032 | bytes 918597 | solution.py:66
  75.0 3.8 copy.79
  78.8 14.9 %fusion.130 = f32[64,64,128]{1,2,0:T(8,128)} fusion(f32[64,64,1]{1,2,0:T(1,128)S(1)} %collective-permute-done.5, f32[64,64,128]{1,2,0:T(8,128)} %copy-done.4, f32[64,64,1]{1,2,0:T(1,128)S(1)} %collective-permute-done.4, f32[1,64,130]{1,2,0:T(8,128)S(1)} %collective-permute-done.7, f32[1,64,130]{1,2,0:T(8,128)S(1)} %collective-permute-done.6, ...), kind=kLoop, calls=%fused_computation.120 | loop fusion | flops 9437184 | bytes 6392064 | tf_op jit(solution)/shard_map/add | solution.py:151
  93.7 5.9 gather_fusion
  99.6 5.9 gather_fusion.1
  105.5 5.9 gather_fusion.2
  111.3 8.3 %gather_fusion.3 = f32[512,64]{1,0:T(8,128)} fusion(f32[64,64,128]{1,2,0:T(8,128)} %fusion.130, s32[512]{0:T(512)S(1)} %get-tuple-element.284), kind=kCustom, calls=%fused_computation.3 | custom fusion | bytes 266240 | tf_op jit(solution)/shard_map/gather | solution.py:113
  123.2 47.5 %all-to-all-start.1 = ((f32[32,1,1024]{2,1,0:T(1,128)}), f32[32,1,1024]{2,1,0:T(1,128)S(1)}, u32[]{:S(2)}, u32[]{:S(2)}) async-start(f32[32,1,1024]{2,1,0:T(1,128)} %reshape.217), calls=%async_computation.1 | async-start | bytes 262144 | tf_op jit(solution)/shard_map/all_to_all | solution.py:157
  170.7 7.7 %all-to-all-done.1 = f32[32,1,1024]{2,1,0:T(1,128)S(1)} async-done(((f32[32,1,1024]{2,1,0:T(1,128)}), f32[32,1,1024]{2,1,0:T(1,128)S(1)}, u32[]{:S(2)}, u32[]{:S(2)}) %all-to-all-start.1) | async-done | bytes 131104 | tf_op jit(solution)/shard_map/all_to_all | solution.py:157
  183.4 10.0 %all_to_all.30 = f32[32,1,1024]{2,1,0:T(1,128)S(1)} all-to-all(f32[32,1,1024]{2,1,0:T(1,128)S(1)} %reshape.219), channel_id=1, replica_groups=mesh['lat'=4,'lon'=8] {'lat','lon'}, dimensions={0} | all-to-all | bytes 262144 | tf_op jit(solution)/shard_map/all_to_all | solution.py:173
  199.3 52.4 %scatter_fusion = f32[64,64,128]{1,2,0:T(8,128)} fusion(f32[64,64,128]{1,2,0:T(8,128)} %broadcast_in_dim.20, s32[512]{0:T(512)S(1)} %get-tuple-element.290, f32[512,64]{1,0:T(8,128)} %bitcast.306), kind=kCustom, calls=%fused_computation.7 | custom fusion | flops 32768 | bytes 397312 | tf_op jit(solution)/shard_map/scatter-add | solution.py:121
  251.8 52.2 %scatter_fusion.1 = f32[64,64,128]{1,2,0:T(8,128)} fusion(f32[64,64,128]{1,2,0:T(8,128)} %scatter_fusion, s32[512]{0:T(512)S(1)} %get-tuple-element.289, f32[512,64]{1,0:T(8,128)S(1)} %bitcast.305), kind=kCustom, calls=%fused_computation.8 | custom fusion | flops 32768 | bytes 397312 | tf_op jit(solution)/shard_map/scatter-add | solution.py:121
  304.0 52.1 %scatter_fusion.2 = f32[64,64,128]{1,2,0:T(8,128)} fusion(f32[64,64,128]{1,2,0:T(8,128)} %scatter_fusion.1, s32[512]{0:T(512)S(1)} %get-tuple-element.288, f32[512,64]{1,0:T(8,128)S(1)} %bitcast.304), kind=kCustom, calls=%fused_computation.9 | custom fusion | flops 32768 | bytes 397312 | tf_op jit(solution)/shard_map/scatter-add | solution.py:121
  356.1 52.1 %scatter_fusion.3 = f32[64,64,128]{1,2,0:T(8,128)} fusion(f32[64,64,128]{1,2,0:T(8,128)} %scatter_fusion.2, s32[512]{0:T(512)S(1)} %get-tuple-element.283, f32[512,64]{1,0:T(8,128)S(1)} %bitcast.303), kind=kCustom, calls=%fused_computation.10 | custom fusion | flops 32768 | bytes 397312 | tf_op jit(solution)/shard_map/scatter-add | solution.py:121
  409.2 44.9 %collective-permute-start.8 = (f32[64,64,1]{1,2,0:T(1,128)S(1)}, f32[64,64,1]{1,2,0:T(1,128)S(1)}, u32[]{:S(2)}, u32[]{:S(2)}) collective-permute-start(f32[64,64,1]{1,2,0:T(1,128)S(1)} %get-tuple-element.358), channel_id=1, source_target_pairs={{0,1},{1,2},{2,3},{3,4},{4,5},{5,6},{6,7},{7,0},{8,9},{9,10},{10,1... | collective-permute-start | bytes 49160 | tf_op jit(solution)/shard_map/ppermute | solution.py:18
  466.1 47.7 %while.52 = (s32[]{:T(128)}, f32[64,512]{1,0:T(8,128)}, f32[512,64]{0,1:T(8,128)}, f32[4,16,64,128]{3,2,1,0:T(8,128)}, bf16[4,16,64,128]{3,2,1,0:T(8,128)(2,1)S(...) while((s32[]{:T(128)}, f32[64,512]{1,0:T(8,128)}, ...), condition=%wide.region_14.15_spmd.clone, body=%wide.region_13.14_spmd.clone.sunk | while | flops 676462592 | bytes 46336196 | solution.py:94
  474.2 3.8 fusion.242
  486.1 3.8 fusion.242
  498.1 3.8 fusion.242
  510.0 3.8 fusion.242
  513.8 3.8 copy.83
  517.7 14.9 %fusion.121 = f32[64,64,128]{1,2,0:T(8,128)} fusion(f32[64,64,128]{1,2,0:T(8,128)} %scatter_fusion.3, f32[64,64,1]{1,2,0:T(1,128)S(1)} %collective-permute-done.8, f32[64,64,1]{1,2,0:T(1,128)S(1)} %collective-permute-done.9, f32[1,64,130]{1,2,0:T(8,128)} %collective-permute-done.11, f32[1,64,130]{1,2,0:T(8,128)} %collective-permute-done.10, ...), kind=kLoop, calls=%fused_computation.103 | loop fusion | flops 9437184 | bytes 6392064 | tf_op jit(solution)/shard_map/add | solution.py:178
  537.5 41.1 %while.53 = (s32[]{:T(128)}, f32[64,512]{1,0:T(8,128)S(1)}, f32[512,64]{0,1:T(8,128)}, f32[4,16,64,128]{3,2,1,0:T(8,128)}, bf16[4,16,64,128]{3,2,1,0:T(8,128)(2,...) while((s32[]{:T(128)}, f32[64,512]{1,0:T(8,128)S(1)}, ...), condition=%wide.region_16.17_spmd.clone, body=%wide.region_15.16_spmd.clone.sunk | while | flops 676462592 | bytes 37947028 | solution.py:94
  595.2 3.8 copy.85
  599.0 53.2 %all-reduce.5.cloned.1.call-done = (f32[64,512]{1,0:T(8,128)}, f32[512,64]{0,1:T(8,128)}) async-done(((f32[64,512]{1,0:T(8,128)}, f32[512,64]{0,1:T(8,128)}), (f32[64,512]{1,0:T(8,128)}, f32[512,64]{0,1:T(8,128)})) %all-reduce.5.cloned.1.call-update) | async-done | bytes 262160 | tf_op jit(solution)/shard_map/psum | solution.py:181
  652.3 14.8 %fusion.112 = f32[64,64,128]{1,2,0:T(8,128)} fusion(f32[64,64,128]{1,2,0:T(8,128)} %fusion.121, f32[64,64,1]{1,2,0:T(1,128)S(1)} %collective-permute-done.12, f32[64,64,1]{1,2,0:T(1,128)S(1)} %collective-permute-done.13, f32[1,64,130]{1,2,0:T(8,128)S(1)} %collective-permute-done.15, f32[1,64,130]{1,2,0:T(8,128)S(1)} %collective-permute-done.14, ...), kind=kLoop, calls=%fused_computation.86 | loop fusion | flops 9437184 | bytes 6392064 | tf_op jit(solution)/shard_map/add | solution.py:180
  667.0 3.8 copy.86
  670.8 15.4 %all-reduce.7.cloned.1.call-done = (f32[64,512]{1,0:T(8,128)}, f32[512,64]{0,1:T(8,128)}) async-done(((f32[64,512]{1,0:T(8,128)}, f32[512,64]{0,1:T(8,128)}), (f32[64,512]{1,0:T(8,128)}, f32[512,64]{0,1:T(8,128)})) %all-reduce.7.cloned.1.call-update) | async-done | bytes 262160 | tf_op jit(solution)/shard_map/psum | solution.py:181
  (207 shorter events, 178.7 us)
Async XLA Ops:
  7.2 173.6 %copy-start = (f32[128,64]{0,1:T(8,128)S(1)}, f32[128,64]{0,1:T(8,128)}, u32[]{:S(2)}) copy-start(f32[128,64]{0,1:T(8,128)} %param.22) | copy-start | bytes 98308
  7.2 17.7 %copy-start.9 = (f32[64,64,128]{2,1,0:T(8,128)S(1)}, f32[64,64,128]{2,1,0:T(8,128)}, u32[]{:S(2)}) copy-start(f32[64,64,128]{2,1,0:T(8,128)} %param.18) | copy-start | bytes 6291460
  11.1 14.2 %copy-start.6 = (bf16[64,512]{1,0:T(8,128)(2,1)S(1)}, bf16[64,512]{1,0:T(8,128)(2,1)}, u32[]{:S(2)}) copy-start(bf16[64,512]{1,0:T(8,128)(2,1)} %param.20) | copy-start | bytes 196612
  11.1 14.2 %copy-start.10 = (bf16[512,64]{0,1:T(8,128)(2,1)S(1)}, bf16[512,64]{0,1:T(8,128)(2,1)}, u32[]{:S(2)}) copy-start(bf16[512,64]{0,1:T(8,128)(2,1)} %param.21) | copy-start | bytes 196612
  12.3 21.6 %collective-permute-start = (f32[64,64,1]{1,2,0:T(1,128)S(1)}, f32[64,64,1]{1,2,0:T(1,128)S(1)}, u32[]{:S(2)}, u32[]{:S(2)}) collective-permute-start(f32[64,64,1]{1,2,0:T(1,128)S(1)} %get-tuple-element.361), channel_id=1, source_target_pairs={{0,1},{1,2},{2,3},{3,4},{4,5},{5,6},{6,7},{7,0},{8,9},{9,10},{10,1... | collective-permute-start | bytes 49160 | tf_op jit(solution)/shard_map/ppermute | solution.py:18
  15.3 18.5 %collective-permute-start.1 = (f32[64,64,1]{1,2,0:T(1,128)S(1)}, f32[64,64,1]{1,2,0:T(1,128)S(1)}, u32[]{:S(2)}, u32[]{:S(2)}) collective-permute-start(f32[64,64,1]{1,2,0:T(1,128)S(1)} %get-tuple-element.362), channel_id=1, source_target_pairs={{1,0},{2,1},{3,2},{4,3},{5,4},{6,5},{7,6},{0,7},{9,8},{10,9},{11,1... | collective-permute-start | bytes 49160 | tf_op jit(solution)/shard_map/ppermute | solution.py:19
  21.6 11.9 %all-to-all-start = ((s32[32,16,4]{1,2,0:T(4,128)}), s32[32,16,4]{1,2,0:T(4,128)S(1)}, u32[]{:S(2)}, u32[]{:S(2)}) async-start(s32[32,16,4]{1,2,0:T(4,128)} %copy.69), calls=%async_computation | async-start | bytes 131072 | tf_op jit(solution)/shard_map/all_to_all | solution.py:145
  30.8 48.0 %copy-start.11 = (f32[64]{0:T(128)}, f32[64]{0:T(128)S(1)}, u32[]{:S(2)}) copy-start(f32[64]{0:T(128)S(1)} %get-tuple-element.374) | copy-start | bytes 772
  30.8 48.0 %copy-start.14 = (f32[64]{0:T(128)}, f32[64]{0:T(128)S(1)}, u32[]{:S(2)}) copy-start(f32[64]{0:T(128)S(1)} %get-tuple-element.375) | copy-start | bytes 772
  34.9 3.8 collective-permute-start.2
  37.2 4.3 collective-permute-start.3
  49.6 8.6 %collective-permute-start.4 = (f32[64,64,1]{1,2,0:T(1,128)S(1)}, f32[64,64,1]{1,2,0:T(1,128)S(1)}, u32[]{:S(2)}, u32[]{:S(2)}) collective-permute-start(f32[64,64,1]{1,2,0:T(1,128)S(1)} %get-tuple-element.359), channel_id=1, source_target_pairs={{0,1},{1,2},{2,3},{3,4},{4,5},{5,6},{6,7},{7,0},{8,9},{9,10},{10,1... | collective-permute-start | bytes 49160 | tf_op jit(solution)/shard_map/ppermute | solution.py:18
  51.1 7.1 %collective-permute-start.5 = (f32[64,64,1]{1,2,0:T(1,128)S(1)}, f32[64,64,1]{1,2,0:T(1,128)S(1)}, u32[]{:S(2)}, u32[]{:S(2)}) collective-permute-start(f32[64,64,1]{1,2,0:T(1,128)S(1)} %get-tuple-element.360), channel_id=1, source_target_pairs={{1,0},{2,1},{3,2},{4,3},{5,4},{6,5},{7,6},{0,7},{9,8},{10,9},{11,1... | collective-permute-start | bytes 49160 | tf_op jit(solution)/shard_map/ppermute | solution.py:19
  59.1 19.7 %collective-permute-start.6 = (f32[1,64,130]{1,2,0:T(8,128)S(1)}, f32[1,64,130]{1,2,0:T(8,128)S(1)}, u32[]{:S(2)}, u32[]{:S(2)}) collective-permute-start(f32[1,64,130]{1,2,0:T(8,128)S(1)} %get-tuple-element.351), channel_id=1, source_target_pairs={{0,8},{8,16},{16,24},{1,9},{9,17},{17,25},{2,10},{10,18},{18,26},{... | collective-permute-start | bytes 99848 | tf_op jit(solution)/shard_map/ppermute | solution.py:18
  63.4 15.3 %collective-permute-start.7 = (f32[1,64,130]{1,2,0:T(8,128)S(1)}, f32[1,64,130]{1,2,0:T(8,128)S(1)}, u32[]{:S(2)}, u32[]{:S(2)}) collective-permute-start(f32[1,64,130]{1,2,0:T(8,128)S(1)} %get-tuple-element.352), channel_id=1, source_target_pairs={{8,0},{16,8},{24,16},{9,1},{17,9},{25,17},{10,2},{18,10},{26,18},{... | collective-permute-start | bytes 99848 | tf_op jit(solution)/shard_map/ppermute | solution.py:19
  105.4 75.3 %copy-start.20 = (f32[256,128]{1,0:T(8,128)S(1)}, f32[256,128]{1,0:T(8,128)}, u32[]{:S(2)}) copy-start(f32[256,128]{1,0:T(8,128)} %param.24) | copy-start | bytes 393220
  105.4 75.3 %copy-start.21 = (s32[256]{0:T(256)S(1)}, s32[256]{0:T(256)}, u32[]{:S(2)}) copy-start(s32[256]{0:T(256)} %param.27) | copy-start | bytes 3076
  105.5 75.3 %copy-start.22 = (f32[128]{0:T(128)S(1)}, f32[128]{0:T(128)}, u32[]{:S(2)}) copy-start(f32[128]{0:T(128)} %param.23) | copy-start | bytes 1540
  123.2 55.3 %all-to-all-start.1 = ((f32[32,1,1024]{2,1,0:T(1,128)}), f32[32,1,1024]{2,1,0:T(1,128)S(1)}, u32[]{:S(2)}, u32[]{:S(2)}) async-start(f32[32,1,1024]{2,1,0:T(1,128)} %reshape.217), calls=%async_computation.1 | async-start | bytes 262144 | tf_op jit(solution)/shard_map/all_to_all | solution.py:157
  170.6 481.6 %all-reduce.5.cloned.1.call-start = ((), (), s32[]{:S(2)}) async-start(), calls=%async_computation.3 | async-start | bytes 524288 | tf_op jit(solution)/shard_map/psum | solution.py:181
  409.2 48.3 %collective-permute-start.8 = (f32[64,64,1]{1,2,0:T(1,128)S(1)}, f32[64,64,1]{1,2,0:T(1,128)S(1)}, u32[]{:S(2)}, u32[]{:S(2)}) collective-permute-start(f32[64,64,1]{1,2,0:T(1,128)S(1)} %get-tuple-element.358), channel_id=1, source_target_pairs={{0,1},{1,2},{2,3},{3,4},{4,5},{5,6},{6,7},{7,0},{8,9},{9,10},{10,1... | collective-permute-start | bytes 49160 | tf_op jit(solution)/shard_map/ppermute | solution.py:18
  454.1 3.9 collective-permute-start.9
  459.5 58.1 %collective-permute-start.10 = (f32[1,64,130]{1,2,0:T(8,128)}, f32[1,64,130]{1,2,0:T(8,128)}, u32[]{:S(2)}, u32[]{:S(2)}) collective-permute-start(f32[1,64,130]{1,2,0:T(8,128)} %get-tuple-element.349), channel_id=1, source_target_pairs={{8,0},{16,8},{24,16},{9,1},{17,9},{25,17},{10,2},{18,10},{26,18},{... | collective-permute-start | bytes 99848 | tf_op jit(solution)/shard_map/ppermute | solution.py:19
  460.8 56.8 %collective-permute-start.11 = (f32[1,64,130]{1,2,0:T(8,128)S(1)}, f32[1,64,130]{1,2,0:T(8,128)}, u32[]{:S(2)}, u32[]{:S(2)}) collective-permute-start(f32[1,64,130]{1,2,0:T(8,128)S(1)} %get-tuple-element.350), channel_id=1, source_target_pairs={{0,8},{8,16},{16,24},{1,9},{9,17},{17,25},{2,10},{10,18},{18,26},{... | collective-permute-start | bytes 99848 | tf_op jit(solution)/shard_map/ppermute | solution.py:18
  581.8 104.5 %all-reduce.7.cloned.1.call-start = ((), (), s32[]{:S(2)}) async-start(), calls=%async_computation.4 | async-start | bytes 524288 | tf_op jit(solution)/shard_map/psum | solution.py:181
  582.9 6.8 collective-permute-start.12
  584.4 5.2 collective-permute-start.13
  590.6 61.7 %copy-start.13 = (f32[64]{0:T(128)S(1)}, f32[64]{0:T(128)}, u32[]{:S(2)}) copy-start(f32[64]{0:T(128)} %copy-done.11) | copy-start | bytes 772
  590.6 61.7 %copy-start.16 = (f32[64]{0:T(128)S(1)}, f32[64]{0:T(128)}, u32[]{:S(2)}) copy-start(f32[64]{0:T(128)} %copy-done.14) | copy-start | bytes 772
  590.6 61.6 %collective-permute-start.14 = (f32[1,64,130]{1,2,0:T(8,128)S(1)}, f32[1,64,130]{1,2,0:T(8,128)S(1)}, u32[]{:S(2)}, u32[]{:S(2)}) collective-permute-start(f32[1,64,130]{1,2,0:T(8,128)S(1)} %get-tuple-element.347), channel_id=1, source_target_pairs={{8,0},{16,8},{24,16},{9,1},{17,9},{25,17},{10,2},{18,10},{26,18},{... | collective-permute-start | bytes 99848 | tf_op jit(solution)/shard_map/ppermute | solution.py:19
  591.9 60.3 %collective-permute-start.15 = (f32[1,64,130]{1,2,0:T(8,128)S(1)}, f32[1,64,130]{1,2,0:T(8,128)S(1)}, u32[]{:S(2)}, u32[]{:S(2)}) collective-permute-start(f32[1,64,130]{1,2,0:T(8,128)S(1)} %get-tuple-element.348), channel_id=1, source_target_pairs={{0,8},{8,16},{16,24},{1,9},{9,17},{17,25},{2,10},{10,18},{18,26},{... | collective-permute-start | bytes 99848 | tf_op jit(solution)/shard_map/ppermute | solution.py:18
  652.3 37.1 %copy-start.1 = (f32[128,64]{0,1:T(8,128)S(1)}, f32[128,64]{0,1:T(8,128)}, u32[]{:S(2)}) copy-start(f32[128,64]{0,1:T(8,128)} %param.22) | copy-start | bytes 98308
  (24 other events, 81.5 us)
Sparse Core Ops, SparseCore 0:
  581.9 70.2 all-reduce.4
  654.6 31.5 all-reduce.6
